TPU v7x, 32 devices: a whole 2x2x4 slice. The times are simulated.
32 devices in a mesh: view: 2 (over x), row: 4 (over z), mat: 4 (over y, core).
Axes of the slice: x: 2, y: 2, z: 4, core: 2. Of those that a mesh axis runs over, the one named last changes fastest.
Arguments:
- volume: float32 [128, 3, 2048], P(('row', 'mat')), may hold values from 0 to 1
- projector: bfloat16 [8, 1024, 2048], P(('view', 'mat')), may hold values from -0.125 to 0.125
- counts: bfloat16 [8, 128, 4, 1024], P(('view', 'mat'), 'row'), may hold values from 0.049804688 to 1
- atten: float32 [4, 3], replicated, may hold values from 0.1 to 1
- newton: bfloat16 [128, 3, 3, 2048], P(('row', 'mat')), may hold values from -0.25 to 0.80078125, as said below
Outputs:
- updated: float32 [128, 3, 2048], P(('row', 'mat'))
Inputs may be any that keep to these rules, and one draw needn't show every extreme that they name: newton is symmetric in its two material dimensions; after rounding to bfloat16 its diagonal lies in 0.2 to 0.80078125 and each off-diagonal entry is at most about 0.3 times the root of the two diagonal entries in magnitude.
All inputs are finite; a program needn't handle non-finite values.
Results may differ from a plain program's by a relative error of at most 0.0028.
The roundings to bfloat16 on the way count: a program that leaves them out, or rounds other values in their place, can miss the bound.
Values may be sent and summed in bfloat16 or wider, within the bound.
A program may use at most 64 MiB of HBM per device.

v0:
```python
import jax
import jax.numpy as jnp
from jax import lax
from jax.sharding import PartitionSpec as P

PX = 1024


def from_behind(array, axis, by):
    count = lax.axis_size(axis)
    pairs = [(i, i + by) for i in range(count) if 0 <= i + by < count]
    return lax.ppermute(array, axis, pairs)


def planar(field):
    column = lax.broadcasted_iota(jnp.int32, field.shape, 2) % PX
    zero_row = jnp.zeros(field.shape[:2] + (PX,), jnp.float32)
    zero_one = jnp.zeros(field.shape[:2] + (1,), jnp.float32)
    next_row = jnp.concatenate([field[:, :, PX:], zero_row], 2)
    next_pix = jnp.concatenate([field[:, :, 1:], zero_one], 2)
    next_pix = jnp.where(column == PX - 1, 0.0, next_pix)
    return (next_row - field, next_pix - field)


def fluxes(lower, upper):
    diff_z = upper - lower
    diff_y, diff_x = planar(lower)
    scale = jnp.sqrt(
        0.25 + jnp.sum(diff_z * diff_z + diff_y * diff_y + diff_x * diff_x, axis=1, keepdims=True)
    )
    return (diff_z / scale, diff_y / scale, diff_x / scale)


def inflow(flux_y, flux_x):
    column = lax.broadcasted_iota(jnp.int32, flux_x.shape, 2) % PX
    zero_row = jnp.zeros(flux_y.shape[:2] + (PX,), jnp.float32)
    zero_one = jnp.zeros(flux_x.shape[:2] + (1,), jnp.float32)
    prev_y = jnp.concatenate([zero_row, flux_y[:, :, :-PX]], 2)
    prev_x = jnp.concatenate([zero_one, flux_x[:, :, :-1]], 2)
    prev_x = jnp.where(column == 0, 0.0, prev_x)
    return prev_y - flux_y + (prev_x - flux_x)


def body(volume, projector, counts, atten, newton):
    views_all = projector.shape[0] * lax.axis_size("view") * lax.axis_size("mat")
    x_half = volume.astype(jnp.bfloat16)
    line = jnp.einsum(
        "zmp,vup->vzmu",
        lax.all_gather(x_half, "mat", axis=0, tiled=True),
        projector,
        preferred_element_type=jnp.float32,
    )
    measured_photon_counts = counts.astype(jnp.float32)
    parts = [None] * line.shape[2]
    for energy_band_index in range(atten.shape[0]):
        exponent_attenuation = atten[energy_band_index, 0] * line[:, :, 0]
        for mat in range(1, line.shape[2]):
            exponent_attenuation = (
                exponent_attenuation + atten[energy_band_index, mat] * line[:, :, mat]
            )
        forward_difference = measured_photon_counts[:, :, energy_band_index] - jnp.exp(
            -exponent_attenuation
        )
        for mat in range(line.shape[2]):
            term = atten[energy_band_index, mat] * forward_difference
            parts[mat] = term if parts[mat] is None else parts[mat] + term
    resid = jnp.stack(parts, 2).astype(jnp.bfloat16)
    shares = lax.psum_scatter(
        jnp.einsum("vzmu,vup->zmp", resid, projector, preferred_element_type=jnp.float32),
        "mat",
        scatter_dimension=0,
        tiled=True,
    )
    own = lax.psum(shares, "view")
    grad = own * float(views_all) ** (-0.5)
    above = from_behind(volume[:1], ("row", "mat"), -1)
    upper = jnp.concatenate([volume[1:], above], 0)
    flux_z, flux_y, flux_x = fluxes(volume, upper)
    below = from_behind(flux_z[-1:], ("row", "mat"), 1)
    prev_z = jnp.concatenate([below, flux_z[:-1]], 0)
    smooth = prev_z - flux_z + inflow(flux_y, flux_x)
    step_dir = grad + 0.5 * smooth
    hess = newton.astype(jnp.float32)
    return volume - jnp.sum(hess * step_dir[:, None], axis=2)


def solution(mesh):
    in_specs = (
        P(("row", "mat"), None, None),
        P(("view", "mat"), None, None),
        P(("view", "mat"), "row", None, None),
        P(),
        P(("row", "mat"), None, None, None),
    )
    out_specs = P(("row", "mat"), None, None)
    return jax.shard_map(body, mesh=mesh, in_specs=in_specs, out_specs=out_specs, check_vma=False)
```

profile of v0, /device:TPU:0, one launch (start us, length us, event | category | flops | bytes accessed | tf_op | source)
XLA Modules:
  0.0 99.9 jit_solution(12702841390047885236)
XLA Ops:
  6.5 0.0 reduce-scatter.2.cloned.1.call-start
  6.5 0.0 copy-start
  6.5 1.1 %slice.122 = f32[1,3,2048]{2,0,1:T(1,128)S(1)} slice(f32[8,3,2048]{2,0,1:T(8,128)} %param.5), slice={[0:1], [0:3], [0:2048]} | slice | bytes 49152 | tf_op jit(solution)/shard_map/slice | solution.py:76
  7.6 1.4 %collective-permute-start = (f32[1,3,2048]{2,0,1:T(1,128)S(1)}, f32[1,3,2048]{2,0,1:T(1,128)S(1)}, u32[]{:S(2)}, u32[]{:S(2)}) collective-permute-start(f32[1,3,2048]{2,0,1:T(1,128)S(1)} %slice.122), channel_id=1, source_target_pairs={{1,0},{2,1},{3,2},{4,3},{5,4},{6,5},{7,6},{8,7},{9,8},{10,9},{11,1... | collective-permute-start | bytes 73736 | tf_op jit(solution)/shard_map/ppermute | solution.py:12
  9.1 1.8 %fusion.24 = (f32[1,1]{1,0:T(1,128)}, f32[1,1]{1,0:T(1,128)}, f32[1,1]{1,0:T(1,128)}, f32[1,1]{1,0:T(1,128)}, f32[1,1]{1,0:T(1,128)}, /*index=5*/f32[1,1]{1,0:T(...) fusion(f32[4,3]{1,0:T(4,128)} %param.8), kind=kLoop, calls=%fused_computation.42 | loop fusion | bytes 96 | tf_op jit(solution)/shard_map/slice | solution.py:59
  10.9 1.0 %copy_convert_fusion = f32[1,32,4,1024]{3,1,2,0:T(8,128)S(1)} fusion(bf16[1,32,4,1024]{3,2,1,0:T(4,128)(2,1)} %param.7), kind=kLoop, calls=%fused_computation.8 | loop fusion | flops 131072 | bytes 786432 | tf_op jit(solution)/shard_map/convert_element_type | solution.py:53
  11.9 0.9 slice.121
  12.9 1.0 %slice.124 = f32[8,3,2047]{2,0,1:T(8,128)S(1)} slice(f32[8,3,2048]{2,0,1:T(8,128)} %param.5), slice={[0:8], [0:3], [1:2048]} | slice | bytes 393024 | tf_op jit(solution)/shard_map/slice | solution.py:20
  13.9 0.9 slice.123
  14.8 0.0 collective-permute-done
  14.8 1.1 %add_reduce_fusion = f32[8,2048]{1,0:T(8,128)S(1)} fusion(f32[8,3,2048]{2,0,1:T(8,128)} %param.5, f32[8,3,1024]{2,0,1:T(8,128)S(1)} %slice.123, f32[8,3,2047]{2,0,1:T(8,128)S(1)} %slice.124, s32[2048]{0:T(1024)S(1)} %get-tuple-element.28, s32[2048]{0:T(1024)S(1)} %get-tuple-element.29, pred[2048]{0:T(1024)(128)(4,1)S(1)} %fusion.22, ...), kind=kLoop, calls=%fused_computation.19 | loop fusion | flops 622592 | bytes 772000 | tf_op jit(solution)/shard_map/reduce_sum | solution.py:29
  15.9 1.1 %fusion.15 = (f32[8,3,2048]{2,0,1:T(8,128)S(1)}, f32[8,3,2048]{2,0,1:T(8,128)S(1)}, f32[8,3,2048]{2,0,1:T(8,128)S(1)}, bf16[8,3,2048]{2,0,1:T(8,128)(2,1)S(1)}) fusion(f32[8,3,2048]{2,0,1:T(8,128)} %param.5, f32[8,3,1024]{2,0,1:T(8,128)S(1)} %slice.123, f32[8,2048]{1,0:T(8,128)S(1)} %add_sqrt_fusion, f32[1,3,2048]{2,0,1:T(1,128)S(1)} %collective-permute-done, ...), kind=kLoop, calls=%fused_computation.29 | loop fusion | flops 540672 | bytes 1460128 | tf_op jit(solution)/shard_map/div | solution.py:31
  17.1 8.6 %all_gather.3 = bf16[32,3,2048]{2,0,1:T(8,128)(2,1)S(1)} all-gather(bf16[8,3,2048]{2,0,1:T(8,128)(2,1)S(1)} %get-tuple-element.15), channel_id=1, replica_groups=mesh['view'=2,'row'=4,'mat'=4] {'mat'}, dimensions={0}, use_global_device_ids=true | all-gather | bytes 491520 | tf_op jit(solution)/shard_map/all_gather | solution.py:49
  25.7 0.0 copy-done
  25.7 1.4 %fusion.4 = f32[1,32,3,1024]{3,1,2,0:T(8,128)S(1)} fusion(bf16[32,3,2048]{2,0,1:T(8,128)(2,1)S(1)} %all_gather.3, bf16[1,1024,2048]{2,1,0:T(8,128)(2,1)S(1)} %copy-done), kind=kOutput, calls=%fused_computation.4 | convolution fusion | flops 402653184 | bytes 4980736 | tf_op jit(solution)/shard_map/zmp,vup->vzmu/dot_general | solution.py:47
  27.1 7.6 %fusion.16 = (bf16[32,1,1024]{2,0,1:T(8,128)(2,1)S(1)}, f32[1,32,1,1024]{3,1,2,0:T(8,128)S(1)}, f32[1,32,1,1024]{3,1,2,0:T(8,128)S(1)}, f32[1,32,1,1024]{3,1,2,0:T(8,128)S(1)}, f32[1,32,1,1024]{3,1,2,0:T(8,128)S(1)}) fusion(f32[]{:T(128)} %bitcast.14, f32[]{:T(128)} %bitcast.11, f32[]{:T(128)} %bitcast.8, f32[]{:T(128)} %bitcast, ...), kind=kLoop, calls=%fused_computation.32 | loop fusion | flops 1179648 | bytes 1507376 | tf_op jit(solution)/shard_map/stack | solution.py:67
  34.8 5.2 %fusion.17 = (bf16[32,1,1024]{2,0,1:T(8,128)(2,1)S(1)}, bf16[32,1,1024]{2,0,1:T(8,128)(2,1)S(1)}) fusion(f32[1,32,1,1024]{3,1,2,0:T(8,128)S(1)} %get-tuple-element.9, f32[1,32,1,1024]{3,1,2,0:T(8,128)S(1)} %get-tuple-element.8, f32[1,32,1,1024]{3,1,2,0:T(8,128)S(1)} %get-tuple-element.7, f32[1,32,1,1024]{3,1,2,0:T(8,128)S(1)} %get-tuple-element.6, ...), kind=kLoop, calls=%fused_computation.33 | loop fusion | flops 524288 | bytes 655392 | tf_op jit(solution)/shard_map/stack | solution.py:67
  39.9 0.0 copy-start.2
  39.9 0.0 copy-start.1
  39.9 1.7 %fusion = f32[32,3,2048]{2,0,1:T(8,128)} fusion(bf16[1,1024,2048]{2,1,0:T(8,128)(2,1)S(1)} %copy-done, bf16[32,1,1024]{2,0,1:T(8,128)(2,1)S(1)} %get-tuple-element.11, bf16[32,1,1024]{2,0,1:T(8,128)(2,1)S(1)} %get-tuple-element.10, bf16[32,1,1024]{2,0,1:T(8,128)(2,1)S(1)} %get-tuple-element.5), kind=kOutput, calls=%fused_computation | convolution fusion | flops 402849792 | bytes 5177344 | tf_op jit(solution)/shard_map/vzmu,vup->zmp/dot_general | solution.py:69
  41.7 0.0 reduce-scatter.2.cloned.1.call-update
  41.7 0.0 all-reduce.6.cloned.1.call-start
  41.7 24.8 %reduce-scatter.2.cloned.1.call-done = f32[8,3,2048]{2,0,1:T(8,128)} async-done(((f32[32,3,2048]{2,0,1:T(8,128)}), f32[8,3,2048]{2,0,1:T(8,128)}) %reduce-scatter.2.cloned.1.call-update) | async-done | bytes 196624 | tf_op jit(solution)/shard_map/reduce_scatter | solution.py:68
  66.5 0.0 all-reduce.6.cloned.1.call-update
  66.5 1.6 %collective-permute-start.1 = (f32[1,3,2048]{2,0,1:T(1,128)S(1)}, f32[1,3,2048]{2,0,1:T(1,128)S(1)}, u32[]{:S(2)}, u32[]{:S(2)}) collective-permute-start(f32[1,3,2048]{2,0,1:T(1,128)S(1)} %slice.136), channel_id=1, source_target_pairs={{0,1},{1,2},{2,3},{3,4},{4,5},{5,6},{6,7},{7,8},{8,9},{9,10},{10,1... | collective-permute-start | bytes 73736 | tf_op jit(solution)/shard_map/ppermute | solution.py:12
  68.1 0.8 collective-permute-done.1
  69.0 22.3 %all-reduce.6.cloned.1.call-done = f32[8,3,2048]{2,0,1:T(8,128)} async-done(((f32[8,3,2048]{2,0,1:T(8,128)}), f32[8,3,2048]{2,0,1:T(8,128)}) %all-reduce.6.cloned.1.call-update) | async-done | bytes 196624 | tf_op jit(solution)/shard_map/psum | solution.py:74
  91.2 1.1 %fusion.14 = f32[8,3,2048]{2,0,1:T(8,128)S(1)} fusion(f32[8,3,2048]{2,0,1:T(8,128)S(1)} %get-tuple-element.13, f32[7,3,2048]{2,0,1:T(8,128)S(1)} %bitcast.33, f32[1,3,2048]{2,0,1:T(1,128)S(1)} %collective-permute-done.1, f32[8,3,2048]{2,0,1:T(8,128)S(1)} %get-tuple-element.14, f32[8,3,2047]{2,0,1:T(8,128)S(1)} %bitcast.34, ...), kind=kLoop, calls=%fused_computation.18 | loop fusion | flops 589824 | bytes 1492896 | tf_op jit(solution)/shard_map/add | solution.py:82
  92.3 0.0 copy-done.2
  92.3 0.1 multiply_reduce_fusion
  92.4 0.0 copy-done.1
  92.4 0.7 sub.71
  (5 shorter events, 0.1 us)
Async XLA Ops:
  6.5 60.0 %reduce-scatter.2.cloned.1.call-start = ((), (), s32[]{:S(2)}) async-start(), calls=%async_computation.1 | async-start | bytes 983040 | tf_op jit(solution)/shard_map/reduce_scatter | solution.py:68
  6.5 19.1 %copy-start = (bf16[1,1024,2048]{2,1,0:T(8,128)(2,1)S(1)}, bf16[1,1024,2048]{2,1,0:T(8,128)(2,1)}, u32[]{:S(2)}) copy-start(bf16[1,1024,2048]{2,1,0:T(8,128)(2,1)} %param.6) | copy-start | bytes 12582916
  7.6 7.2 %collective-permute-start = (f32[1,3,2048]{2,0,1:T(1,128)S(1)}, f32[1,3,2048]{2,0,1:T(1,128)S(1)}, u32[]{:S(2)}, u32[]{:S(2)}) collective-permute-start(f32[1,3,2048]{2,0,1:T(1,128)S(1)} %slice.122), channel_id=1, source_target_pairs={{1,0},{2,1},{3,2},{4,3},{5,4},{6,5},{7,6},{8,7},{9,8},{10,9},{11,1... | collective-permute-start | bytes 73736 | tf_op jit(solution)/shard_map/ppermute | solution.py:12
  39.9 52.4 %copy-start.2 = (bf16[8,3,3,2048]{3,0,2,1:T(8,128)(2,1)S(1)}, bf16[8,3,3,2048]{3,0,2,1:T(8,128)(2,1)}, u32[]{:S(2)}) copy-start(bf16[8,3,3,2048]{3,0,2,1:T(8,128)(2,1)} %param.9) | copy-start | bytes 884740
  39.9 52.5 %copy-start.1 = (f32[8,3,2048]{2,0,1:T(8,128)S(1)}, f32[8,3,2048]{2,0,1:T(8,128)}, u32[]{:S(2)}) copy-start(f32[8,3,2048]{2,0,1:T(8,128)} %param.5) | copy-start | bytes 589828
  41.7 49.5 %all-reduce.6.cloned.1.call-start = ((), (), s32[]{:S(2)}) async-start(), calls=%async_computation.2 | async-start | bytes 393216 | tf_op jit(solution)/shard_map/psum | solution.py:74
  66.5 2.4 %collective-permute-start.1 = (f32[1,3,2048]{2,0,1:T(1,128)S(1)}, f32[1,3,2048]{2,0,1:T(1,128)S(1)}, u32[]{:S(2)}, u32[]{:S(2)}) collective-permute-start(f32[1,3,2048]{2,0,1:T(1,128)S(1)} %slice.136), channel_id=1, source_target_pairs={{0,1},{1,2},{2,3},{3,4},{4,5},{5,6},{6,7},{7,8},{8,9},{9,10},{10,1... | collective-permute-start | bytes 73736 | tf_op jit(solution)/shard_map/ppermute | solution.py:12
Sparse Core Ops, SparseCore 0:
  41.8 24.6 reduce-scatter.1
  68.8 22.4 all-reduce.5
where the time goes:
time: 100 us; the launch traced here: 99.9 us
  waiting for transfers between devices  47.9 us (48%)
  other arithmetic  17.9 us (18%)
  between operations  13.6 us (14%)
  blocking collectives  8.61 us (9%)
  local copies, waits for them, and re-layouts  5.83 us (6%)
  matrix products  3.15 us (3%)
  starting transfers between devices  3.04 us (3%)
    reduce_scatter x1, waiting for transfers between devices, body(): lax.psum_scatter(jnp.einsum('vzmu,vup->zmp', resid, projector, preferred_...  24.8 us
    psum x1, waiting for transfers between devices, body(): own = lax.psum(shares, 'view')  22.3 us
    another operation x2, other arithmetic, body(): resid = jnp.stack(parts, 2).astype(jnp.bfloat16)  12.8 us
    all_gather x1, blocking collectives, body(): lax.all_gather(x_half, 'mat', axis=0, tiled=True)  8.61 us
    ppermute x2, starting transfers between devices, from_behind(): return lax.ppermute(array, axis, pairs)  3 us
  transfers between devices with their start and end apart: 4, of which 3 were waited for; matrix products, arithmetic and copies ran while one was open for 6% of the time, Pallas kernels for 0%

commit v1 on v0

v1 whole, which is shorter than its diff:
```python
import functools

import jax
import jax.numpy as jnp
from jax import lax
from jax.experimental import pallas as pl
from jax.experimental.pallas import tpu as pltpu
from jax.sharding import PartitionSpec as P

PX = 1024
CHUNKS = 4
MESH = pl.DeviceIdType.MESH
F32 = jnp.float32
BF16 = jnp.bfloat16


def shift_rows(field, by):
    zero = jnp.zeros((field.shape[0], PX), F32)
    if by > 0:
        return jnp.concatenate([zero, field[:, :-PX]], 1)
    return jnp.concatenate([field[:, PX:], zero], 1)


def shift_pix(field, by):
    size = field.shape[1]
    column = lax.broadcasted_iota(jnp.int32, field.shape, 1) % PX
    rolled = pltpu.roll(field, by % size, 1)
    edge = 0 if by > 0 else PX - 1
    return jnp.where(column == edge, 0.0, rolled)


def kernel(dims, vol_hbm, vt_hbm, proj_hbm, cnt_hbm, nw_hbm, atten, out,
           vt, proj, cnt, nw, halo, xs, acc, res, base, g0, s1, r1, s2, r2, r3,
           loc_sem, proj_sem, halo_s, halo_r, agp_s, agp_r, agy_s, agy_r, agf_s, agf_r,
           rs1_s, rs1_r, rs2_s, rs2_r, rs3_s, rs3_r):
    views, rows, mats, mat_count, bins, depth, width, views_all = dims
    half = mats // 2
    v, r, i = lax.axis_index("view"), lax.axis_index("row"), lax.axis_index("mat")
    par = i % 2
    group = i // 2
    pair = (v, r, i + 1 - 2 * par)
    peers = [None] + [(v, r, 2 * lax.rem(group + d, half) + par) for d in range(1, half)]
    others = [None] + [(lax.rem(v + d, views), r, i) for d in range(1, views)]
    slab = r * mats + i
    slabs = rows * mats
    up, down = lax.rem(slab + 1, slabs), lax.rem(slab + slabs - 1, slabs)
    above = (v, up // mats, up % mats)
    below = (v, down // mats, down % mats)

    barrier = pltpu.get_barrier_semaphore()
    greet = [pair, above, below] + peers[1:] + others[1:]
    for device in greet:
        pl.semaphore_signal(barrier, inc=1, device_id=device, device_id_type=MESH)

    load_vol = pltpu.make_async_copy(vt_hbm, vt, loc_sem.at[0])
    load_vol.start()
    load_proj = []
    for c in range(CHUNKS):
        cols = pl.ds(c * width, width)
        load_proj.append(pltpu.make_async_copy(proj_hbm.at[0, :, cols], proj.at[:, cols], proj_sem.at[c]))
        load_proj[c].start()
    load_cnt = pltpu.make_async_copy(cnt_hbm, cnt, loc_sem.at[1])
    load_cnt.start()
    load_nw = pltpu.make_async_copy(nw_hbm, nw, loc_sem.at[2])
    load_nw.start()

    load_vol.wait()
    for c in range(CHUNKS):
        cols = slice(c * width, (c + 1) * width)
        xs[c, 0] = jnp.concatenate([vt[m, :, cols] for m in range(mat_count)], 0).astype(BF16)
    pl.semaphore_wait(barrier, len(greet))

    def send(src, dst, s, t, device):
        copy = pltpu.make_async_remote_copy(src, dst, s, t, device_id=device, device_id_type=MESH)
        copy.start()
        return copy

    agy = [[None] * half for c in range(CHUNKS)]
    agp = []
    for c in range(CHUNKS):
        for d in range(1, half):
            agy[c][d] = send(xs.at[c, 0], xs.at[c, 2 * (half - d)], agy_s.at[c, d - 1],
                             agy_r.at[c, half - d - 1], peers[d])
        agp.append(send(xs.at[c, 0], xs.at[c, 1], agp_s.at[c], agp_r.at[c], pair))
    to_below = send(vol_hbm.at[0], halo.at[0], halo_s.at[0], halo_r.at[0], below)
    to_above = send(vol_hbm.at[depth - 1], halo.at[1], halo_s.at[1], halo_r.at[1], above)

    to_below.wait_recv()
    to_above.wait_recv()
    load_nw.wait()
    z = lax.broadcasted_iota(jnp.int32, vt.shape[1:], 0)
    last, first = slab == slabs - 1, slab == 0
    cur = [vt[m] for m in range(mat_count)]
    after = [jnp.where(z == depth - 1, jnp.where(last, 0.0, halo[0, m:m + 1, :]), pltpu.roll(cur[m], depth - 1, 0))
             for m in range(mat_count)]
    before = [jnp.where(z == 0, halo[1, m:m + 1, :], pltpu.roll(cur[m], 1, 0)) for m in range(mat_count)]

    def fluxes(lower, upper):
        dz = [b - a for a, b in zip(lower, upper)]
        dy = [shift_rows(a, -1) - a for a in lower]
        dx = [shift_pix(a, -1) - a for a in lower]
        total = 0.25
        for m in range(mat_count):
            total = total + (dz[m] * dz[m] + dy[m] * dy[m] + dx[m] * dx[m])
        scale = 1.0 / jnp.sqrt(total)
        return [a * scale for a in dz], [a * scale for a in dy], [a * scale for a in dx]

    qz, qy, qx = fluxes(cur, after)
    pz, _, _ = fluxes(before, cur)
    tv = []
    for m in range(mat_count):
        prev_z = jnp.where(jnp.logical_and(first, z == 0), 0.0, pz[m])
        tv.append(0.5 * ((prev_z - qz[m]) + (shift_rows(qy[m], 1) - qy[m]) + (shift_pix(qx[m], 1) - qx[m])))
    for m in range(mat_count):
        total = nw[m, 0].astype(F32) * tv[0]
        for k in range(1, mat_count):
            total = total + nw[m, k].astype(F32) * tv[k]
        base[m] = cur[m] - total

    agf = [[None] * half for c in range(CHUNKS)]
    for c in range(CHUNKS):
        for d in range(1, half):
            agy[c][half - d].wait_recv()
            agf[c][d] = send(xs.at[c, 2 * d], xs.at[c, 2 * d + 1], agf_s.at[c, d - 1], agf_r.at[c, d - 1], pair)
    for c in range(CHUNKS):
        load_proj[c].wait()
        agp[c].wait_recv()
        for d in range(1, half):
            agf[c][d].wait_recv()
        x = jnp.concatenate([xs[c, s] for s in range(mats)], 0)
        part = lax.dot_general(x, proj[:, c * width:(c + 1) * width], (((1,), (1,)), ((), ())),
                               preferred_element_type=F32)
        if c == 0:
            acc[...] = part
        else:
            acc[...] += part

    load_cnt.wait()
    span = mat_count * depth
    for s in range(mats):
        owner = 2 * lax.rem(group + s // 2, half) + (par if s % 2 == 0 else 1 - par)
        line = [acc[s * span + m * depth:s * span + (m + 1) * depth, :] for m in range(mat_count)]
        parts = [None] * mat_count
        for b in range(bins):
            expo = atten[b, 0] * line[0]
            for m in range(1, mat_count):
                expo = expo + atten[b, m] * line[m]
            diff = cnt[owner, b].astype(F32) - jnp.exp(-expo)
            for m in range(mat_count):
                term = atten[b, m] * diff
                parts[m] = term if parts[m] is None else parts[m] + term
        res[s] = jnp.concatenate(parts, 0).astype(BF16)

    rs1 = []
    resid = jnp.concatenate([res[s] for s in range(mats)], 0)
    for c in range(CHUNKS):
        part = jnp.dot(resid, proj[:, c * width:(c + 1) * width], preferred_element_type=F32)
        for d in range(half):
            s1[c, d] = part[(2 * d + 1) * span:(2 * d + 2) * span].astype(BF16)
            g0[c, d] = part[2 * d * span:(2 * d + 1) * span]
        rs1.append(send(s1.at[c], r1.at[c], rs1_s.at[c], rs1_r.at[c], pair))
    rs2 = [[None] * half for c in range(CHUNKS)]
    for c in range(CHUNKS):
        rs1[c].wait_recv()
        for d in range(1, half):
            s2[c, d - 1] = (g0[c, d] + r1[c, d].astype(F32)).astype(BF16)
            rs2[c][d] = send(s2.at[c, d - 1], r2.at[c, half - d - 1], rs2_s.at[c, d - 1],
                             rs2_r.at[c, half - d - 1], peers[d])
        g0[c, 0] = g0[c, 0] + r1[c, 0].astype(F32)
    rs3 = [[None] * views for c in range(CHUNKS)]
    for c in range(CHUNKS):
        total = g0[c, 0]
        for d in range(1, half):
            rs2[c][half - d].wait_recv()
            total = total + r2[c, d - 1].astype(F32)
        r3[c, v] = total.astype(BF16)
        for d in range(1, views):
            rs3[c][d] = send(r3.at[c, v], r3.at[c, v], rs3_s.at[c, d - 1], rs3_r.at[c, views - d - 1], others[d])
    for c in range(CHUNKS):
        cols = slice(c * width, (c + 1) * width)
        for d in range(1, views):
            source = lax.rem(v + views - d, views)
            pltpu.make_async_remote_copy(r3.at[c, source], r3.at[c, source], rs3_s.at[c, d - 1],
                                         rs3_r.at[c, views - d - 1], device_id=others[d],
                                         device_id_type=MESH).wait_recv()
        grad = r3[c, 0].astype(F32)
        for w in range(1, views):
            grad = grad + r3[c, w].astype(F32)
        grad = grad * float(views_all) ** (-0.5)
        for m in range(mat_count):
            total = nw[m, 0, :, cols].astype(F32) * grad[:depth]
            for k in range(1, mat_count):
                total = total + nw[m, k, :, cols].astype(F32) * grad[k * depth:(k + 1) * depth]
            out[m, :, cols] = base[m, :, cols] - total

    to_below.wait_send()
    to_above.wait_send()
    for c in range(CHUNKS):
        agp[c].wait_send()
        rs1[c].wait_send()
        for d in range(1, half):
            agy[c][d].wait_send()
            agf[c][d].wait_send()
            rs2[c][d].wait_send()
        for d in range(1, views):
            rs3[c][d].wait_send()


def body(volume, projector, counts, atten, newton):
    views, rows, mats = (lax.axis_size(a) for a in ("view", "row", "mat"))
    depth, mat_count, pixels = volume.shape
    columns = projector.shape[1]
    bins = atten.shape[0]
    views_all = projector.shape[0] * views * mats
    width = pixels // CHUNKS
    half = mats // 2
    span = depth * mat_count
    vol_t = jnp.transpose(volume, (1, 0, 2))
    cnt_t = jnp.transpose(counts.reshape(mats, depth, bins, columns), (0, 2, 1, 3))
    nw_t = jnp.transpose(newton, (1, 2, 0, 3))
    dims = (views, rows, mats, mat_count, bins, depth, width, views_all)
    any_spec = pl.BlockSpec(memory_space=pl.ANY)
    dma = pltpu.SemaphoreType.DMA
    out = pl.pallas_call(
        functools.partial(kernel, dims),
        out_shape=jax.ShapeDtypeStruct((mat_count, depth, pixels), F32),
        in_specs=[any_spec] * 5 + [pl.BlockSpec(memory_space=pltpu.SMEM)],
        out_specs=pl.BlockSpec(memory_space=pltpu.VMEM),
        scratch_shapes=[
            pltpu.VMEM((mat_count, depth, pixels), F32),
            pltpu.VMEM((columns, pixels), BF16),
            pltpu.VMEM((mats, bins, depth, columns), BF16),
            pltpu.VMEM((mat_count, mat_count, depth, pixels), BF16),
            pltpu.VMEM((2, mat_count, pixels), F32),
            pltpu.VMEM((CHUNKS, mats, span, width), BF16),
            pltpu.VMEM((mats * span, columns), F32),
            pltpu.VMEM((mats, span, columns), BF16),
            pltpu.VMEM((mat_count, depth, pixels), F32),
            pltpu.VMEM((CHUNKS, half, span, width), F32),
            pltpu.VMEM((CHUNKS, half, span, width), BF16),
            pltpu.VMEM((CHUNKS, half, span, width), BF16),
            pltpu.VMEM((CHUNKS, half - 1, span, width), BF16),
            pltpu.VMEM((CHUNKS, half - 1, span, width), BF16),
            pltpu.VMEM((CHUNKS, views, span, width), BF16),
            dma((3,)), dma((CHUNKS,)), dma((2,)), dma((2,)),
            dma((CHUNKS,)), dma((CHUNKS,)),
            dma((CHUNKS, half - 1)), dma((CHUNKS, half - 1)),
            dma((CHUNKS, half - 1)), dma((CHUNKS, half - 1)),
            dma((CHUNKS,)), dma((CHUNKS,)),
            dma((CHUNKS, half - 1)), dma((CHUNKS, half - 1)),
            dma((CHUNKS, views - 1)), dma((CHUNKS, views - 1)),
        ],
        compiler_params=pltpu.CompilerParams(
            collective_id=0, has_side_effects=True, vmem_limit_bytes=48 * 1024 * 1024
        ),
    )(volume, vol_t, projector, cnt_t, nw_t, atten)
    return jnp.transpose(out, (1, 0, 2))


def solution(mesh):
    in_specs = (
        P(("row", "mat"), None, None),
        P(("view", "mat"), None, None),
        P(("view", "mat"), "row", None, None),
        P(),
        P(("row", "mat"), None, None, None),
    )
    out_specs = P(("row", "mat"), None, None)
    return jax.shard_map(body, mesh=mesh, in_specs=in_specs, out_specs=out_specs, check_vma=False)
```

time: 100 us -> 28.7 us (0.29)
  waiting for transfers between devices: 47.9 us -> 0 us
  Pallas kernels: 0 us -> 20.8 us
  other arithmetic: 17.9 us -> 0 us
  between operations: 13.6 us -> 0.03 us
  blocking collectives: 8.61 us -> 0 us
  matrix products: 3.15 us -> 0 us
  starting transfers between devices: 3.04 us -> 0 us
  local copies, waits for them, and re-layouts: 5.83 us -> 7.53 us
    reduce_scatter x1 -> x0, waiting for transfers between devices: 24.8 us -> none  [body(): lax.psum_scatter(jnp.einsum('vzmu,vup->zmp', resid, projector, preferred_...]
    psum x1 -> x0, waiting for transfers between devices: 22.3 us -> none  [body(): own = lax.psum(shares, 'view')]
    pallas_call x0 -> x1, Pallas kernels: none -> 20.8 us  [body(): pl.pallas_call(functools.partial(kernel, dims), out_shape=jax.ShapeDtypeS...]
    another operation x2 -> x0, other arithmetic: 12.8 us -> none  [body(): resid = jnp.stack(parts, 2).astype(jnp.bfloat16)]
    all_gather x1 -> x0, blocking collectives: 8.61 us -> none  [body(): lax.all_gather(x_half, 'mat', axis=0, tiled=True)]
    unnamed x6 -> x10, local copies, waits for them, and re-layouts: 0.02 us -> 6.5 us
    slice x7 -> x0, local copies, waits for them, and re-layouts: 5.82 us -> none  [the longest x1 1.81 us: body(): atten[energy_band_index, mat] * line[:, :, mat]]
    dot_general x2 -> x0, matrix products: 3.15 us -> none  [the longest x1 1.7 us: body(): jnp.einsum('vzmu,vup->zmp', resid, projector, preferred_element_type=jnp....]
  transfers between devices with their start and end apart: 4 -> 0, of which waited for: 3 -> 0; matrix products, arithmetic and copies ran while one was open for 6% -> 0% of each run, Pallas kernels for 0% -> 0%
where the time goes in v1:
time: 28.7 us; the launch traced here: 28.4 us
  Pallas kernels  20.8 us (72%)
  local copies, waits for them, and re-layouts  7.53 us (26%)
    pallas_call x1, Pallas kernels, body(): pl.pallas_call(functools.partial(kernel, dims), out_shape=jax.ShapeDtypeS...  20.8 us
    unnamed x10, local copies, waits for them, and re-layouts  6.5 us
    reshape x1, local copies, waits for them, and re-layouts, body(): counts.reshape(mats, depth, bins, columns)  1.03 us

profile of v1, /device:TPU:0, one launch (start us, length us, event | category | flops | bytes accessed | tf_op | source)
XLA Modules:
  0.0 28.4 jit_solution(431305321202865279)
XLA Ops:
  0.0 1.0 %copy.13 = bf16[4,8,4,1024]{3,1,2,0:T(8,128)(2,1)S(1)} copy(bf16[4,8,4,1024]{3,2,1,0:T(4,128)(2,1)} %bitcast.11) | data formatting | bytes 524288 | tf_op jit(solution)/shard_map/reshape | solution.py:219
  1.0 1.1 %copy.9.vol_hbm = f32[8,3,2048]{2,1,0:T(4,128)S(1)} copy(f32[8,3,2048]{2,0,1:T(8,128)} %param.5) | data formatting | bytes 393216 | tf_op args[0]
  2.1 0.0 copy-start
  2.1 2.2 %copy-done = bf16[1,1024,2048]{2,1,0:T(8,128)(2,1)S(1)} copy-done((bf16[1,1024,2048]{2,1,0:T(8,128)(2,1)S(1)}, bf16[1,1024,2048]{2,1,0:T(8,128)(2,1)}, u32[]{:S(2)}) %copy-start) | copy-done | bytes 4194328
  4.3 0.0 copy-start.1
  4.3 0.9 %copy-done.1 = f32[8,3,2048]{2,0,1:T(8,128)S(1)} copy-done((f32[8,3,2048]{2,0,1:T(8,128)S(1)}, f32[8,3,2048]{2,0,1:T(8,128)}, u32[]{:S(2)}) %copy-start.1) | copy-done | bytes 196632
  5.2 0.0 copy-start.2
  5.2 1.0 %copy-done.2 = bf16[8,3,3,2048]{3,0,2,1:T(8,128)(2,1)S(1)} copy-done((bf16[8,3,3,2048]{3,0,2,1:T(8,128)(2,1)S(1)}, bf16[8,3,3,2048]{3,0,2,1:T(8,128)(2,1)}, u32[]{:S(2)}) %copy-start.2) | copy-done | bytes 294936
  6.2 0.0 copy-start.3
  6.2 0.7 %copy-done.3 = f32[4,3]{1,0:T(4,128)S(1)} copy-done((f32[4,3]{1,0:T(4,128)S(1)}, f32[4,3]{1,0:T(4,128)}, u32[]{:S(2)}) %copy-start.3) | copy-done | bytes 72
  6.9 20.8 %shard_map.55 = f32[3,8,2048]{2,1,0:T(8,128)S(1)} custom-call(f32[8,3,2048]{2,1,0:T(4,128)S(1)} %copy.9.vol_hbm, f32[3,8,2048]{2,1,0:T(8,128)S(1)} %bitcast.8, bf16[1,1024,2048]{2,1,0:T(8,128)(2,1)S(1)} %copy-done, bf16[4,4,8,1024]{3,2,1,0:T(8,128)(2,1)S(1)} %bitcast.7, bf16[3,3,8,2048]{3,2,1,0:T(8,128)(2,1)S(1)} %bitcast.10, f32[4,3]{1,0:T(4,128)S(1)} %copy-done.3), custom_call_target="tpu_custom_call" | custom-call | tf_op jit(solution)/shard_map/pallas_call | solution.py:224
  27.7 0.7 %copy.15 = f32[8,3,2048]{2,0,1:T(8,128)} copy(f32[8,3,2048]{2,0,1:T(8,128)S(1)} %bitcast.9) | data formatting | bytes 393216
Async XLA Ops:
  2.1 2.2 %copy-start = (bf16[1,1024,2048]{2,1,0:T(8,128)(2,1)S(1)}, bf16[1,1024,2048]{2,1,0:T(8,128)(2,1)}, u32[]{:S(2)}) copy-start(bf16[1,1024,2048]{2,1,0:T(8,128)(2,1)} %proj_hbm.1) | copy-start | bytes 12582916
  4.3 0.9 %copy-start.1 = (f32[8,3,2048]{2,0,1:T(8,128)S(1)}, f32[8,3,2048]{2,0,1:T(8,128)}, u32[]{:S(2)}) copy-start(f32[8,3,2048]{2,0,1:T(8,128)} %param.5) | copy-start | bytes 589828
  5.2 1.0 %copy-start.2 = (bf16[8,3,3,2048]{3,0,2,1:T(8,128)(2,1)S(1)}, bf16[8,3,3,2048]{3,0,2,1:T(8,128)(2,1)}, u32[]{:S(2)}) copy-start(bf16[8,3,3,2048]{3,0,2,1:T(8,128)(2,1)} %param.9) | copy-start | bytes 884740
  6.2 0.7 %copy-start.3 = (f32[4,3]{1,0:T(4,128)S(1)}, f32[4,3]{1,0:T(4,128)}, u32[]{:S(2)}) copy-start(f32[4,3]{1,0:T(4,128)} %atten.1) | copy-start | bytes 148

commit v2 on v1

--- a/solution.py
+++ b/solution.py
@@ -29,8 +29,8 @@
     return jnp.where(column == edge, 0.0, rolled)
 
 
-def kernel(dims, vol_hbm, vt_hbm, proj_hbm, cnt_hbm, nw_hbm, atten, out,
-           vt, proj, cnt, nw, halo, xs, acc, res, base, g0, s1, r1, s2, r2, r3,
+def kernel(dims, vt_hbm, proj_hbm, cnt_hbm, nw_hbm, atten_hbm, out,
+           vt, proj, cnt_in, cnt, nw, atten, edge, halo, xs, acc, res, base, g0, s1, r1, s2, r2, r3,
            loc_sem, proj_sem, halo_s, halo_r, agp_s, agp_r, agy_s, agy_r, agf_s, agf_r,
            rs1_s, rs1_r, rs2_s, rs2_r, rs3_s, rs3_r):
     views, rows, mats, mat_count, bins, depth, width, views_all = dims
@@ -59,12 +59,16 @@
         cols = pl.ds(c * width, width)
         load_proj.append(pltpu.make_async_copy(proj_hbm.at[0, :, cols], proj.at[:, cols], proj_sem.at[c]))
         load_proj[c].start()
-    load_cnt = pltpu.make_async_copy(cnt_hbm, cnt, loc_sem.at[1])
+    load_cnt = pltpu.make_async_copy(cnt_hbm, cnt_in, loc_sem.at[1])
+    load_att = pltpu.make_async_copy(atten_hbm, atten, loc_sem.at[3])
+    load_att.start()
     load_cnt.start()
     load_nw = pltpu.make_async_copy(nw_hbm, nw, loc_sem.at[2])
     load_nw.start()
 
     load_vol.wait()
+    edge[0] = jnp.concatenate([vt[m, 0:1, :] for m in range(mat_count)], 0)
+    edge[1] = jnp.concatenate([vt[m, depth - 1:depth, :] for m in range(mat_count)], 0)
     for c in range(CHUNKS):
         cols = slice(c * width, (c + 1) * width)
         xs[c, 0] = jnp.concatenate([vt[m, :, cols] for m in range(mat_count)], 0).astype(BF16)
@@ -82,8 +86,8 @@
             agy[c][d] = send(xs.at[c, 0], xs.at[c, 2 * (half - d)], agy_s.at[c, d - 1],
                              agy_r.at[c, half - d - 1], peers[d])
         agp.append(send(xs.at[c, 0], xs.at[c, 1], agp_s.at[c], agp_r.at[c], pair))
-    to_below = send(vol_hbm.at[0], halo.at[0], halo_s.at[0], halo_r.at[0], below)
-    to_above = send(vol_hbm.at[depth - 1], halo.at[1], halo_s.at[1], halo_r.at[1], above)
+    to_below = send(edge.at[0], halo.at[0], halo_s.at[0], halo_r.at[0], below)
+    to_above = send(edge.at[1], halo.at[1], halo_s.at[1], halo_r.at[1], above)
 
     to_below.wait_recv()
     to_above.wait_recv()
@@ -117,6 +121,13 @@
             total = total + nw[m, k].astype(F32) * tv[k]
         base[m] = cur[m] - total
 
+    load_att.wait()
+    load_cnt.wait()
+    for j in range(mats):
+        tiles = [cnt_in[j, a].astype(F32) for a in range(depth)]
+        for b in range(bins):
+            cnt[j, b] = jnp.concatenate([tile[b:b + 1] for tile in tiles], 0)
+
     agf = [[None] * half for c in range(CHUNKS)]
     for c in range(CHUNKS):
         for d in range(1, half):
@@ -135,7 +146,6 @@
         else:
             acc[...] += part
 
-    load_cnt.wait()
     span = mat_count * depth
     for s in range(mats):
         owner = 2 * lax.rem(group + s // 2, half) + (par if s % 2 == 0 else 1 - par)
@@ -145,7 +155,7 @@
             expo = atten[b, 0] * line[0]
             for m in range(1, mat_count):
                 expo = expo + atten[b, m] * line[m]
-            diff = cnt[owner, b].astype(F32) - jnp.exp(-expo)
+            diff = cnt[owner, b] - jnp.exp(-expo)
             for m in range(mat_count):
                 term = atten[b, m] * diff
                 parts[m] = term if parts[m] is None else parts[m] + term
@@ -216,21 +226,24 @@
     half = mats // 2
     span = depth * mat_count
     vol_t = jnp.transpose(volume, (1, 0, 2))
-    cnt_t = jnp.transpose(counts.reshape(mats, depth, bins, columns), (0, 2, 1, 3))
+    cnt = counts.reshape(mats, depth, bins, columns)
     nw_t = jnp.transpose(newton, (1, 2, 0, 3))
     dims = (views, rows, mats, mat_count, bins, depth, width, views_all)
-    any_spec = pl.BlockSpec(memory_space=pl.ANY)
+    hbm = pl.BlockSpec(memory_space=pltpu.HBM)
     dma = pltpu.SemaphoreType.DMA
     out = pl.pallas_call(
         functools.partial(kernel, dims),
         out_shape=jax.ShapeDtypeStruct((mat_count, depth, pixels), F32),
-        in_specs=[any_spec] * 5 + [pl.BlockSpec(memory_space=pltpu.SMEM)],
+        in_specs=[hbm] * 5,
         out_specs=pl.BlockSpec(memory_space=pltpu.VMEM),
         scratch_shapes=[
             pltpu.VMEM((mat_count, depth, pixels), F32),
             pltpu.VMEM((columns, pixels), BF16),
-            pltpu.VMEM((mats, bins, depth, columns), BF16),
+            pltpu.VMEM((mats, depth, bins, columns), BF16),
+            pltpu.VMEM((mats, bins, depth, columns), F32),
             pltpu.VMEM((mat_count, mat_count, depth, pixels), BF16),
+            pltpu.SMEM(atten.shape, F32),
+            pltpu.VMEM((2, mat_count, pixels), F32),
             pltpu.VMEM((2, mat_count, pixels), F32),
             pltpu.VMEM((CHUNKS, mats, span, width), BF16),
             pltpu.VMEM((mats * span, columns), F32),
@@ -242,7 +255,7 @@
             pltpu.VMEM((CHUNKS, half - 1, span, width), BF16),
             pltpu.VMEM((CHUNKS, half - 1, span, width), BF16),
             pltpu.VMEM((CHUNKS, views, span, width), BF16),
-            dma((3,)), dma((CHUNKS,)), dma((2,)), dma((2,)),
+            dma((4,)), dma((CHUNKS,)), dma((2,)), dma((2,)),
             dma((CHUNKS,)), dma((CHUNKS,)),
             dma((CHUNKS, half - 1)), dma((CHUNKS, half - 1)),
             dma((CHUNKS, half - 1)), dma((CHUNKS, half - 1)),
@@ -251,9 +264,9 @@
             dma((CHUNKS, views - 1)), dma((CHUNKS, views - 1)),
         ],
         compiler_params=pltpu.CompilerParams(
-            collective_id=0, has_side_effects=True, vmem_limit_bytes=48 * 1024 * 1024
+            collective_id=0, has_side_effects=True, vmem_limit_bytes=67043328
         ),
-    )(volume, vol_t, projector, cnt_t, nw_t, atten)
+    )(vol_t, projector, cnt, nw_t, atten)
     return jnp.transpose(out, (1, 0, 2))
 
 

time: 28.7 us -> 22.6 us (0.79)
  local copies, waits for them, and re-layouts: 7.53 us -> 1.62 us
    unnamed x10 -> x1, local copies, waits for them, and re-layouts: 6.5 us -> 1.62 us
    reshape x1 -> x0, local copies, waits for them, and re-layouts: 1.03 us -> none  [body(): counts.reshape(mats, depth, bins, columns)]
where the time goes in v2:
time: 22.6 us; the launch traced here: 22.4 us
  Pallas kernels  20.8 us (92%)
  local copies, waits for them, and re-layouts  1.62 us (7%)
    pallas_call x1, Pallas kernels, body(): pl.pallas_call(functools.partial(kernel, dims), out_shape=jax.ShapeDtypeS...  20.8 us
    unnamed x1, local copies, waits for them, and re-layouts  1.62 us

profile of v2, /device:TPU:0, one launch (start us, length us, event | category | flops | bytes accessed | tf_op | source)
XLA Modules:
  0.0 22.4 jit_solution(13694957882393831358)
XLA Ops:
  0.0 20.8 %shard_map.55 = f32[3,8,2048]{2,1,0:T(8,128)} custom-call(f32[3,8,2048]{2,1,0:T(8,128)} %bitcast.7, bf16[1,1024,2048]{2,1,0:T(8,128)(2,1)} %proj_hbm.1, bf16[4,8,4,1024]{3,2,1,0:T(4,128)(2,1)} %bitcast.6, bf16[3,3,8,2048]{3,2,1,0:T(8,128)(2,1)} %bitcast.5, f32[4,3]{1,0:T(4,128)} %atten_hbm.1), custom_call_target="tpu_custom_call" | custom-call | tf_op jit(solution)/shard_map/pallas_call | solution.py:234
  20.8 1.6 %copy.7 = f32[8,3,2048]{2,0,1:T(8,128)} copy(f32[8,3,2048]{2,0,1:T(8,128)} %bitcast.4) | data formatting | bytes 393216

commit v3 on v2

--- a/solution.py
+++ b/solution.py
@@ -8,7 +8,8 @@
 from jax.sharding import PartitionSpec as P
 
 PX = 1024
-CHUNKS = 4
+CHUNKS = 8
+ROOM = 208 * 1024
 MESH = pl.DeviceIdType.MESH
 F32 = jnp.float32
 BF16 = jnp.bfloat16
@@ -31,7 +32,7 @@
 
 def kernel(dims, vt_hbm, proj_hbm, cnt_hbm, nw_hbm, atten_hbm, out,
            vt, proj, cnt_in, cnt, nw, atten, edge, halo, xs, acc, res, base, g0, s1, r1, s2, r2, r3,
-           loc_sem, proj_sem, halo_s, halo_r, agp_s, agp_r, agy_s, agy_r, agf_s, agf_r,
+           loc_sem, vol_sem, proj_sem, halo_s, halo_r, agp_s, agp_r, agy_s, agy_r, agf_s, agf_r,
            rs1_s, rs1_r, rs2_s, rs2_r, rs3_s, rs3_r):
     views, rows, mats, mat_count, bins, depth, width, views_all = dims
     half = mats // 2
@@ -48,12 +49,24 @@
     below = (v, down // mats, down % mats)
 
     barrier = pltpu.get_barrier_semaphore()
-    greet = [pair, above, below] + peers[1:] + others[1:]
+    last, first = slab == slabs - 1, slab == 0
+    greet = [pair] + peers[1:] + others[1:]
     for device in greet:
         pl.semaphore_signal(barrier, inc=1, device_id=device, device_id_type=MESH)
 
-    load_vol = pltpu.make_async_copy(vt_hbm, vt, loc_sem.at[0])
-    load_vol.start()
+    @pl.when(jnp.logical_not(first))
+    def _():
+        pl.semaphore_signal(barrier, inc=1, device_id=below, device_id_type=MESH)
+
+    @pl.when(jnp.logical_not(last))
+    def _():
+        pl.semaphore_signal(barrier, inc=1, device_id=above, device_id_type=MESH)
+
+    load_vol = []
+    for c in range(CHUNKS):
+        cols = pl.ds(c * width, width)
+        load_vol.append(pltpu.make_async_copy(vt_hbm.at[:, :, cols], vt.at[:, :, cols], vol_sem.at[c]))
+        load_vol[c].start()
     load_proj = []
     for c in range(CHUNKS):
         cols = pl.ds(c * width, width)
@@ -66,60 +79,43 @@
     load_nw = pltpu.make_async_copy(nw_hbm, nw, loc_sem.at[2])
     load_nw.start()
 
-    load_vol.wait()
-    edge[0] = jnp.concatenate([vt[m, 0:1, :] for m in range(mat_count)], 0)
-    edge[1] = jnp.concatenate([vt[m, depth - 1:depth, :] for m in range(mat_count)], 0)
-    for c in range(CHUNKS):
-        cols = slice(c * width, (c + 1) * width)
-        xs[c, 0] = jnp.concatenate([vt[m, :, cols] for m in range(mat_count)], 0).astype(BF16)
-    pl.semaphore_wait(barrier, len(greet))
-
     def send(src, dst, s, t, device):
         copy = pltpu.make_async_remote_copy(src, dst, s, t, device_id=device, device_id_type=MESH)
         copy.start()
         return copy
 
+    def halo_copy(way, device):
+        return pltpu.make_async_remote_copy(edge.at[way], halo.at[way], halo_s.at[way], halo_r.at[way],
+                                            device_id=device, device_id_type=MESH)
+
+    to_below, to_above = halo_copy(0, below), halo_copy(1, above)
     agy = [[None] * half for c in range(CHUNKS)]
     agp = []
     for c in range(CHUNKS):
+        cols = slice(c * width, (c + 1) * width)
+        if c == 0:
+            load_vol[c].wait()
+        xs[c, 0] = jnp.concatenate([vt[m, :, cols] for m in range(mat_count)], 0).astype(BF16)
+        if c == 0:
+            ends = jnp.where(first, 1, 0) + jnp.where(last, 1, 0)
+            pl.semaphore_wait(barrier, len(greet) + 2 - ends)
         for d in range(1, half):
             agy[c][d] = send(xs.at[c, 0], xs.at[c, 2 * (half - d)], agy_s.at[c, d - 1],
                              agy_r.at[c, half - d - 1], peers[d])
         agp.append(send(xs.at[c, 0], xs.at[c, 1], agp_s.at[c], agp_r.at[c], pair))
-    to_below = send(edge.at[0], halo.at[0], halo_s.at[0], halo_r.at[0], below)
-    to_above = send(edge.at[1], halo.at[1], halo_s.at[1], halo_r.at[1], above)
-
-    to_below.wait_recv()
-    to_above.wait_recv()
-    load_nw.wait()
-    z = lax.broadcasted_iota(jnp.int32, vt.shape[1:], 0)
-    last, first = slab == slabs - 1, slab == 0
-    cur = [vt[m] for m in range(mat_count)]
-    after = [jnp.where(z == depth - 1, jnp.where(last, 0.0, halo[0, m:m + 1, :]), pltpu.roll(cur[m], depth - 1, 0))
-             for m in range(mat_count)]
-    before = [jnp.where(z == 0, halo[1, m:m + 1, :], pltpu.roll(cur[m], 1, 0)) for m in range(mat_count)]
-
-    def fluxes(lower, upper):
-        dz = [b - a for a, b in zip(lower, upper)]
-        dy = [shift_rows(a, -1) - a for a in lower]
-        dx = [shift_pix(a, -1) - a for a in lower]
-        total = 0.25
-        for m in range(mat_count):
-            total = total + (dz[m] * dz[m] + dy[m] * dy[m] + dx[m] * dx[m])
-        scale = 1.0 / jnp.sqrt(total)
-        return [a * scale for a in dz], [a * scale for a in dy], [a * scale for a in dx]
-
-    qz, qy, qx = fluxes(cur, after)
-    pz, _, _ = fluxes(before, cur)
-    tv = []
-    for m in range(mat_count):
-        prev_z = jnp.where(jnp.logical_and(first, z == 0), 0.0, pz[m])
-        tv.append(0.5 * ((prev_z - qz[m]) + (shift_rows(qy[m], 1) - qy[m]) + (shift_pix(qx[m], 1) - qx[m])))
-    for m in range(mat_count):
-        total = nw[m, 0].astype(F32) * tv[0]
-        for k in range(1, mat_count):
-            total = total + nw[m, k].astype(F32) * tv[k]
-        base[m] = cur[m] - total
+        if c == 0:
+            for rest in load_vol[1:]:
+                rest.wait()
+            edge[0] = jnp.concatenate([vt[m, 0:1, :] for m in range(mat_count)], 0)
+            edge[1] = jnp.concatenate([vt[m, depth - 1:depth, :] for m in range(mat_count)], 0)
+
+            @pl.when(jnp.logical_not(first))
+            def _():
+                to_below.start()
+
+            @pl.when(jnp.logical_not(last))
+            def _():
+                to_above.start()
 
     load_att.wait()
     load_cnt.wait()
@@ -128,12 +124,60 @@
         for b in range(bins):
             cnt[j, b] = jnp.concatenate([tile[b:b + 1] for tile in tiles], 0)
 
+    def regularise():
+        @pl.when(jnp.logical_not(last))
+        def _():
+            to_below.wait_recv()
+
+        @pl.when(last)
+        def _():
+            halo[0] = jnp.zeros(halo.shape[1:], F32)
+
+        @pl.when(jnp.logical_not(first))
+        def _():
+            to_above.wait_recv()
+
+        @pl.when(first)
+        def _():
+            halo[1] = jnp.zeros(halo.shape[1:], F32)
+
+        load_nw.wait()
+        z = lax.broadcasted_iota(jnp.int32, vt.shape[1:], 0)
+        cur = [vt[m] for m in range(mat_count)]
+        after = [jnp.where(z == depth - 1, halo[0, m:m + 1, :], pltpu.roll(cur[m], depth - 1, 0))
+                 for m in range(mat_count)]
+        before = [jnp.where(z == 0, halo[1, m:m + 1, :], pltpu.roll(cur[m], 1, 0)) for m in range(mat_count)]
+
+        def fluxes(lower, upper):
+            dz = [b - a for a, b in zip(lower, upper)]
+            dy = [shift_rows(a, -1) - a for a in lower]
+            dx = [shift_pix(a, -1) - a for a in lower]
+            total = 0.25
+            for m in range(mat_count):
+                total = total + (dz[m] * dz[m] + dy[m] * dy[m] + dx[m] * dx[m])
+            scale = 1.0 / jnp.sqrt(total)
+            return [a * scale for a in dz], [a * scale for a in dy], [a * scale for a in dx]
+
+        qz, qy, qx = fluxes(cur, after)
+        pz, _, _ = fluxes(before, cur)
+        tv = []
+        for m in range(mat_count):
+            prev_z = jnp.where(jnp.logical_and(first, z == 0), 0.0, pz[m])
+            tv.append(0.5 * ((prev_z - qz[m]) + (shift_rows(qy[m], 1) - qy[m]) + (shift_pix(qx[m], 1) - qx[m])))
+        for m in range(mat_count):
+            total = nw[m, 0].astype(F32) * tv[0]
+            for k in range(1, mat_count):
+                total = total + nw[m, k].astype(F32) * tv[k]
+            base[m] = cur[m] - total
+
     agf = [[None] * half for c in range(CHUNKS)]
-    for c in range(CHUNKS):
+
+    def relay(c):
         for d in range(1, half):
             agy[c][half - d].wait_recv()
             agf[c][d] = send(xs.at[c, 2 * d], xs.at[c, 2 * d + 1], agf_s.at[c, d - 1], agf_r.at[c, d - 1], pair)
-    for c in range(CHUNKS):
+
+    def forward(c):
         load_proj[c].wait()
         agp[c].wait_recv()
         for d in range(1, half):
@@ -145,6 +189,16 @@
             acc[...] = part
         else:
             acc[...] += part
+
+    lag = CHUNKS // 2
+    for c in range(CHUNKS):
+        relay(c)
+        if c == 0:
+            regularise()
+        if c >= lag:
+            forward(c - lag)
+    for c in range(CHUNKS - lag, CHUNKS):
+        forward(c)
 
     span = mat_count * depth
     for s in range(mats):
@@ -203,8 +257,14 @@
                 total = total + nw[m, k, :, cols].astype(F32) * grad[k * depth:(k + 1) * depth]
             out[m, :, cols] = base[m, :, cols] - total
 
-    to_below.wait_send()
-    to_above.wait_send()
+    @pl.when(jnp.logical_not(first))
+    def _():
+        to_below.wait_send()
+
+    @pl.when(jnp.logical_not(last))
+    def _():
+        to_above.wait_send()
+
     for c in range(CHUNKS):
         agp[c].wait_send()
         rs1[c].wait_send()
@@ -255,7 +315,7 @@
             pltpu.VMEM((CHUNKS, half - 1, span, width), BF16),
             pltpu.VMEM((CHUNKS, half - 1, span, width), BF16),
             pltpu.VMEM((CHUNKS, views, span, width), BF16),
-            dma((4,)), dma((CHUNKS,)), dma((2,)), dma((2,)),
+            dma((4,)), dma((CHUNKS,)), dma((CHUNKS,)), dma((2,)), dma((2,)),
             dma((CHUNKS,)), dma((CHUNKS,)),
             dma((CHUNKS, half - 1)), dma((CHUNKS, half - 1)),
             dma((CHUNKS, half - 1)), dma((CHUNKS, half - 1)),
@@ -264,7 +324,7 @@
             dma((CHUNKS, views - 1)), dma((CHUNKS, views - 1)),
         ],
         compiler_params=pltpu.CompilerParams(
-            collective_id=0, has_side_effects=True, vmem_limit_bytes=67043328
+            collective_id=0, has_side_effects=True, vmem_limit_bytes=67043328 - ROOM
         ),
     )(vol_t, projector, cnt, nw_t, atten)
     return jnp.transpose(out, (1, 0, 2))

time: 22.6 us -> 23.2 us (1.027)
  Pallas kernels: 20.8 us -> 21.4 us
    pallas_call x1, Pallas kernels: 20.8 us -> 21.4 us  [body(): pl.pallas_call(functools.partial(kernel, dims), out_shape=jax.ShapeDtypeS...]
where the time goes in v3:
time: 23.2 us; the launch traced here: 23.1 us
  Pallas kernels  21.4 us (92%)
  local copies, waits for them, and re-layouts  1.62 us (7%)
    pallas_call x1, Pallas kernels, body(): pl.pallas_call(functools.partial(kernel, dims), out_shape=jax.ShapeDtypeS...  21.4 us
    unnamed x1, local copies, waits for them, and re-layouts  1.62 us

profile of v3, /device:TPU:0, one launch (start us, length us, event | category | flops | bytes accessed | tf_op | source)
XLA Modules:
  0.0 23.1 jit_solution(15949729823107829251)
XLA Ops:
  0.0 21.4 %shard_map.55 = f32[3,8,2048]{2,1,0:T(8,128)} custom-call(f32[3,8,2048]{2,1,0:T(8,128)} %bitcast.7, bf16[1,1024,2048]{2,1,0:T(8,128)(2,1)} %proj_hbm.1, bf16[4,8,4,1024]{3,2,1,0:T(4,128)(2,1)} %bitcast.6, bf16[3,3,8,2048]{3,2,1,0:T(8,128)(2,1)} %bitcast.5, f32[4,3]{1,0:T(4,128)} %atten_hbm.1), custom_call_target="tpu_custom_call" | custom-call | tf_op jit(solution)/shard_map/pallas_call | solution.py:294
  21.4 1.6 %copy.7 = f32[8,3,2048]{2,0,1:T(8,128)} copy(f32[8,3,2048]{2,0,1:T(8,128)} %bitcast.4) | data formatting | bytes 393216

commit v4 on v3

--- a/solution.py
+++ b/solution.py
@@ -8,7 +8,8 @@
 from jax.sharding import PartitionSpec as P
 
 PX = 1024
-CHUNKS = 8
+CHUNKS = 4
+PARTS = 4
 ROOM = 208 * 1024
 MESH = pl.DeviceIdType.MESH
 F32 = jnp.float32
@@ -34,7 +35,7 @@
            vt, proj, cnt_in, cnt, nw, atten, edge, halo, xs, acc, res, base, g0, s1, r1, s2, r2, r3,
            loc_sem, vol_sem, proj_sem, halo_s, halo_r, agp_s, agp_r, agy_s, agy_r, agf_s, agf_r,
            rs1_s, rs1_r, rs2_s, rs2_r, rs3_s, rs3_r):
-    views, rows, mats, mat_count, bins, depth, width, views_all = dims
+    views, rows, mats, mat_count, bins, depth, width, piece, views_all = dims
     half = mats // 2
     v, r, i = lax.axis_index("view"), lax.axis_index("row"), lax.axis_index("mat")
     par = i % 2
@@ -217,22 +218,22 @@
 
     rs1 = []
     resid = jnp.concatenate([res[s] for s in range(mats)], 0)
-    for c in range(CHUNKS):
-        part = jnp.dot(resid, proj[:, c * width:(c + 1) * width], preferred_element_type=F32)
+    for c in range(PARTS):
+        part = jnp.dot(resid, proj[:, c * piece:(c + 1) * piece], preferred_element_type=F32)
         for d in range(half):
             s1[c, d] = part[(2 * d + 1) * span:(2 * d + 2) * span].astype(BF16)
             g0[c, d] = part[2 * d * span:(2 * d + 1) * span]
         rs1.append(send(s1.at[c], r1.at[c], rs1_s.at[c], rs1_r.at[c], pair))
-    rs2 = [[None] * half for c in range(CHUNKS)]
-    for c in range(CHUNKS):
+    rs2 = [[None] * half for c in range(PARTS)]
+    for c in range(PARTS):
         rs1[c].wait_recv()
         for d in range(1, half):
             s2[c, d - 1] = (g0[c, d] + r1[c, d].astype(F32)).astype(BF16)
             rs2[c][d] = send(s2.at[c, d - 1], r2.at[c, half - d - 1], rs2_s.at[c, d - 1],
                              rs2_r.at[c, half - d - 1], peers[d])
         g0[c, 0] = g0[c, 0] + r1[c, 0].astype(F32)
-    rs3 = [[None] * views for c in range(CHUNKS)]
-    for c in range(CHUNKS):
+    rs3 = [[None] * views for c in range(PARTS)]
+    for c in range(PARTS):
         total = g0[c, 0]
         for d in range(1, half):
             rs2[c][half - d].wait_recv()
@@ -240,8 +241,8 @@
         r3[c, v] = total.astype(BF16)
         for d in range(1, views):
             rs3[c][d] = send(r3.at[c, v], r3.at[c, v], rs3_s.at[c, d - 1], rs3_r.at[c, views - d - 1], others[d])
-    for c in range(CHUNKS):
-        cols = slice(c * width, (c + 1) * width)
+    for c in range(PARTS):
+        cols = slice(c * piece, (c + 1) * piece)
         for d in range(1, views):
             source = lax.rem(v + views - d, views)
             pltpu.make_async_remote_copy(r3.at[c, source], r3.at[c, source], rs3_s.at[c, d - 1],
@@ -267,10 +268,12 @@
 
     for c in range(CHUNKS):
         agp[c].wait_send()
-        rs1[c].wait_send()
         for d in range(1, half):
             agy[c][d].wait_send()
             agf[c][d].wait_send()
+    for c in range(PARTS):
+        rs1[c].wait_send()
+        for d in range(1, half):
             rs2[c][d].wait_send()
         for d in range(1, views):
             rs3[c][d].wait_send()
@@ -283,17 +286,18 @@
     bins = atten.shape[0]
     views_all = projector.shape[0] * views * mats
     width = pixels // CHUNKS
+    piece = pixels // PARTS
     half = mats // 2
     span = depth * mat_count
     vol_t = jnp.transpose(volume, (1, 0, 2))
     cnt = counts.reshape(mats, depth, bins, columns)
     nw_t = jnp.transpose(newton, (1, 2, 0, 3))
-    dims = (views, rows, mats, mat_count, bins, depth, width, views_all)
+    dims = (views, rows, mats, mat_count, bins, depth, width, piece, views_all)
     hbm = pl.BlockSpec(memory_space=pltpu.HBM)
     dma = pltpu.SemaphoreType.DMA
     out = pl.pallas_call(
         functools.partial(kernel, dims),
-        out_shape=jax.ShapeDtypeStruct((mat_count, depth, pixels), F32),
+        out_shape=pltpu.VMEM((mat_count, depth, pixels), F32),
         in_specs=[hbm] * 5,
         out_specs=pl.BlockSpec(memory_space=pltpu.VMEM),
         scratch_shapes=[
@@ -309,19 +313,19 @@
             pltpu.VMEM((mats * span, columns), F32),
             pltpu.VMEM((mats, span, columns), BF16),
             pltpu.VMEM((mat_count, depth, pixels), F32),
-            pltpu.VMEM((CHUNKS, half, span, width), F32),
-            pltpu.VMEM((CHUNKS, half, span, width), BF16),
-            pltpu.VMEM((CHUNKS, half, span, width), BF16),
-            pltpu.VMEM((CHUNKS, half - 1, span, width), BF16),
-            pltpu.VMEM((CHUNKS, half - 1, span, width), BF16),
-            pltpu.VMEM((CHUNKS, views, span, width), BF16),
+            pltpu.VMEM((PARTS, half, span, piece), F32),
+            pltpu.VMEM((PARTS, half, span, piece), BF16),
+            pltpu.VMEM((PARTS, half, span, piece), BF16),
+            pltpu.VMEM((PARTS, half - 1, span, piece), BF16),
+            pltpu.VMEM((PARTS, half - 1, span, piece), BF16),
+            pltpu.VMEM((PARTS, views, span, piece), BF16),
             dma((4,)), dma((CHUNKS,)), dma((CHUNKS,)), dma((2,)), dma((2,)),
             dma((CHUNKS,)), dma((CHUNKS,)),
             dma((CHUNKS, half - 1)), dma((CHUNKS, half - 1)),
             dma((CHUNKS, half - 1)), dma((CHUNKS, half - 1)),
-            dma((CHUNKS,)), dma((CHUNKS,)),
-            dma((CHUNKS, half - 1)), dma((CHUNKS, half - 1)),
-            dma((CHUNKS, views - 1)), dma((CHUNKS, views - 1)),
+            dma((PARTS,)), dma((PARTS,)),
+            dma((PARTS, half - 1)), dma((PARTS, half - 1)),
+            dma((PARTS, views - 1)), dma((PARTS, views - 1)),
         ],
         compiler_params=pltpu.CompilerParams(
             collective_id=0, has_side_effects=True, vmem_limit_bytes=67043328 - ROOM

time: 23.2 us -> 19.7 us (0.85)
  Pallas kernels: 21.4 us -> 18.9 us
  local copies, waits for them, and re-layouts: 1.62 us -> 0.68 us
    pallas_call x1, Pallas kernels: 21.4 us -> 18.9 us  [body(): pl.pallas_call(functools.partial(kernel, dims), out_shape=pltpu.VMEM((mat...]
    unnamed x1, local copies, waits for them, and re-layouts: 1.62 us -> 0.68 us
where the time goes in v4:
time: 19.7 us; the launch traced here: 19.6 us
  Pallas kernels  18.9 us (96%)
  local copies, waits for them, and re-layouts  0.68 us (3%)
    pallas_call x1, Pallas kernels, body(): pl.pallas_call(functools.partial(kernel, dims), out_shape=pltpu.VMEM((mat...  18.9 us
    unnamed x1, local copies, waits for them, and re-layouts  0.68 us

profile of v4, /device:TPU:0, one launch (start us, length us, event | category | flops | bytes accessed | tf_op | source)
XLA Modules:
  0.0 19.6 jit_solution(17139288042669120942)
XLA Ops:
  0.0 18.9 %shard_map.55 = f32[3,8,2048]{2,1,0:T(8,128)S(1)} custom-call(f32[3,8,2048]{2,1,0:T(8,128)} %bitcast.7, bf16[1,1024,2048]{2,1,0:T(8,128)(2,1)} %proj_hbm.1, bf16[4,8,4,1024]{3,2,1,0:T(4,128)(2,1)} %bitcast.6, bf16[3,3,8,2048]{3,2,1,0:T(8,128)(2,1)} %bitcast.5, f32[4,3]{1,0:T(4,128)} %atten_hbm.1), custom_call_target="tpu_custom_call" | custom-call | tf_op jit(solution)/shard_map/pallas_call | solution.py:298
  18.9 0.7 %copy.7 = f32[8,3,2048]{2,0,1:T(8,128)} copy(f32[8,3,2048]{2,0,1:T(8,128)S(1)} %bitcast.4) | data formatting | bytes 393216

commit v5 on v4

--- a/solution.py
+++ b/solution.py
@@ -10,6 +10,7 @@
 PX = 1024
 CHUNKS = 4
 PARTS = 4
+BEHIND = 2
 ROOM = 208 * 1024
 MESH = pl.DeviceIdType.MESH
 F32 = jnp.float32
@@ -94,8 +95,7 @@
     agp = []
     for c in range(CHUNKS):
         cols = slice(c * width, (c + 1) * width)
-        if c == 0:
-            load_vol[c].wait()
+        load_vol[c].wait()
         xs[c, 0] = jnp.concatenate([vt[m, :, cols] for m in range(mat_count)], 0).astype(BF16)
         if c == 0:
             ends = jnp.where(first, 1, 0) + jnp.where(last, 1, 0)
@@ -104,19 +104,16 @@
             agy[c][d] = send(xs.at[c, 0], xs.at[c, 2 * (half - d)], agy_s.at[c, d - 1],
                              agy_r.at[c, half - d - 1], peers[d])
         agp.append(send(xs.at[c, 0], xs.at[c, 1], agp_s.at[c], agp_r.at[c], pair))
-        if c == 0:
-            for rest in load_vol[1:]:
-                rest.wait()
-            edge[0] = jnp.concatenate([vt[m, 0:1, :] for m in range(mat_count)], 0)
-            edge[1] = jnp.concatenate([vt[m, depth - 1:depth, :] for m in range(mat_count)], 0)
-
-            @pl.when(jnp.logical_not(first))
-            def _():
-                to_below.start()
-
-            @pl.when(jnp.logical_not(last))
-            def _():
-                to_above.start()
+    edge[0] = jnp.concatenate([vt[m, 0:1, :] for m in range(mat_count)], 0)
+    edge[1] = jnp.concatenate([vt[m, depth - 1:depth, :] for m in range(mat_count)], 0)
+
+    @pl.when(jnp.logical_not(first))
+    def _():
+        to_below.start()
+
+    @pl.when(jnp.logical_not(last))
+    def _():
+        to_above.start()
 
     load_att.wait()
     load_cnt.wait()
@@ -194,8 +191,6 @@
     lag = CHUNKS // 2
     for c in range(CHUNKS):
         relay(c)
-        if c == 0:
-            regularise()
         if c >= lag:
             forward(c - lag)
     for c in range(CHUNKS - lag, CHUNKS):
@@ -216,25 +211,39 @@
                 parts[m] = term if parts[m] is None else parts[m] + term
         res[s] = jnp.concatenate(parts, 0).astype(BF16)
 
-    rs1 = []
+    rs1 = [[None] * half for c in range(PARTS)]
+
+    def swap(c, d):
+        rs1[c][d] = send(s1.at[c, d], r1.at[c, d], rs1_s.at[c, d], rs1_r.at[c, d], pair)
+
+    rs2 = [[None] * half for c in range(PARTS)]
+
+    def across(c):
+        for d in range(1, half):
+            rs1[c][d].wait_recv()
+            s2[c, d - 1] = (g0[c, d] + r1[c, d].astype(F32)).astype(BF16)
+            rs2[c][d] = send(s2.at[c, d - 1], r2.at[c, half - d - 1], rs2_s.at[c, d - 1],
+                             rs2_r.at[c, half - d - 1], peers[d])
+
     resid = jnp.concatenate([res[s] for s in range(mats)], 0)
     for c in range(PARTS):
         part = jnp.dot(resid, proj[:, c * piece:(c + 1) * piece], preferred_element_type=F32)
         for d in range(half):
             s1[c, d] = part[(2 * d + 1) * span:(2 * d + 2) * span].astype(BF16)
             g0[c, d] = part[2 * d * span:(2 * d + 1) * span]
-        rs1.append(send(s1.at[c], r1.at[c], rs1_s.at[c], rs1_r.at[c], pair))
-    rs2 = [[None] * half for c in range(PARTS)]
-    for c in range(PARTS):
-        rs1[c].wait_recv()
-        for d in range(1, half):
-            s2[c, d - 1] = (g0[c, d] + r1[c, d].astype(F32)).astype(BF16)
-            rs2[c][d] = send(s2.at[c, d - 1], r2.at[c, half - d - 1], rs2_s.at[c, d - 1],
-                             rs2_r.at[c, half - d - 1], peers[d])
-        g0[c, 0] = g0[c, 0] + r1[c, 0].astype(F32)
+        for d in range(1, half):
+            swap(c, d)
+        if c >= BEHIND:
+            across(c - BEHIND)
+    for c in range(PARTS - BEHIND, PARTS):
+        across(c)
+    for c in range(PARTS):
+        swap(c, 0)
+    regularise()
     rs3 = [[None] * views for c in range(PARTS)]
     for c in range(PARTS):
-        total = g0[c, 0]
+        rs1[c][0].wait_recv()
+        total = g0[c, 0] + r1[c, 0].astype(F32)
         for d in range(1, half):
             rs2[c][half - d].wait_recv()
             total = total + r2[c, d - 1].astype(F32)
@@ -272,8 +281,9 @@
             agy[c][d].wait_send()
             agf[c][d].wait_send()
     for c in range(PARTS):
-        rs1[c].wait_send()
-        for d in range(1, half):
+        rs1[c][0].wait_send()
+        for d in range(1, half):
+            rs1[c][d].wait_send()
             rs2[c][d].wait_send()
         for d in range(1, views):
             rs3[c][d].wait_send()
@@ -323,7 +333,7 @@
             dma((CHUNKS,)), dma((CHUNKS,)),
             dma((CHUNKS, half - 1)), dma((CHUNKS, half - 1)),
             dma((CHUNKS, half - 1)), dma((CHUNKS, half - 1)),
-            dma((PARTS,)), dma((PARTS,)),
+            dma((PARTS, half)), dma((PARTS, half)),
             dma((PARTS, half - 1)), dma((PARTS, half - 1)),
             dma((PARTS, views - 1)), dma((PARTS, views - 1)),
         ],

time: 19.7 us -> 19.4 us (0.985)
  Pallas kernels: 18.9 us -> 18.6 us
    pallas_call x1, Pallas kernels: 18.9 us -> 18.6 us  [body(): pl.pallas_call(functools.partial(kernel, dims), out_shape=pltpu.VMEM((mat...]
where the time goes in v5:
time: 19.4 us; the launch traced here: 19.2 us
  Pallas kernels  18.6 us (96%)
  local copies, waits for them, and re-layouts  0.68 us (4%)
    pallas_call x1, Pallas kernels, body(): pl.pallas_call(functools.partial(kernel, dims), out_shape=pltpu.VMEM((mat...  18.6 us
    unnamed x1, local copies, waits for them, and re-layouts  0.68 us

profile of v5, /device:TPU:0, one launch (start us, length us, event | category | flops | bytes accessed | tf_op | source)
XLA Modules:
  0.0 19.2 jit_solution(15653115040469611809)
XLA Ops:
  0.0 18.6 %shard_map.55 = f32[3,8,2048]{2,1,0:T(8,128)S(1)} custom-call(f32[3,8,2048]{2,1,0:T(8,128)} %bitcast.7, bf16[1,1024,2048]{2,1,0:T(8,128)(2,1)} %proj_hbm.1, bf16[4,8,4,1024]{3,2,1,0:T(4,128)(2,1)} %bitcast.6, bf16[3,3,8,2048]{3,2,1,0:T(8,128)(2,1)} %bitcast.5, f32[4,3]{1,0:T(4,128)} %atten_hbm.1), custom_call_target="tpu_custom_call" | custom-call | tf_op jit(solution)/shard_map/pallas_call | solution.py:308
  18.6 0.7 %copy.7 = f32[8,3,2048]{2,0,1:T(8,128)} copy(f32[8,3,2048]{2,0,1:T(8,128)S(1)} %bitcast.4) | data formatting | bytes 393216
